TPU v7x, 32 devices: a whole 2x2x4 slice. The times are simulated.
32 devices in a mesh: ckpt: 8 (over y, x, core), vocab: 4 (over z).
Axes of the slice: x: 2, y: 2, z: 4, core: 2. Of those that a mesh axis runs over, the one named last changes fastest.
Arguments:
- hidden_rows: bfloat16 [8, 128, 768], P('ckpt'), may hold values from -8 to 8
- norm_gain: float32 [8, 768], P('ckpt'), may hold values from 0.5 to 1.5
- norm_bias: float32 [8, 768], P('ckpt'), may hold values from -1.2 to 1.2
- unembed: bfloat16 [8, 768, 50304], P('ckpt', None, 'vocab'), may hold values from -6 to 6
- target_ids: int32 [128], replicated, may hold values from 0 to 50303
- ckpt_steps: int32 [8], replicated, may hold values from 0 to 143000
- components: int32 [1], replicated, may hold values from 1 to 8
Outputs:
- loadings: bfloat16 [8, 128, 50304], P(None, 'ckpt', 'vocab')
- gram: float32 [8, 8], replicated
- target_logprob: float32 [8, 128], P('ckpt')
All inputs are finite; a program needn't handle non-finite values.
Results may differ from a plain program's by a relative error of at most 0.0063.
Values may be sent and summed in bfloat16 or wider, within the bound.
A program may use at most 192 MiB of HBM per device.

v0:
```python
import functools

import jax
import jax.numpy as jnp
from jax import lax
from jax.experimental import pallas as pl
from jax.experimental.pallas import tpu as pltpu
from jax.sharding import PartitionSpec as P

COMPONENTS = 8
LANES = 128
HIGH = lax.Precision.HIGHEST
MESH = pl.DeviceIdType.MESH
LOW = -1e30
NT = (((1,), (1,)), ((), ()))


def split_tiles(width):
    tiles = -(-width // LANES)
    best = tiles
    for per in range(1, tiles + 1):
        if tiles % per == 0 and per >= 6:
            best = per
            break
    return best * LANES, tiles // best


def spread_steps(steps_ref, shape):
    lane_owner = lax.broadcasted_iota(jnp.int32, shape, 1) % steps_ref.shape[0]
    out = jnp.zeros(shape, jnp.float32)
    for c in range(steps_ref.shape[0]):
        out = jnp.where(lane_owner == c, steps_ref[c].astype(jnp.float32), out)
    return out


def gather_kernel(
    sizes,
    hidden_hbm, gain_hbm, bias_hbm, ids_hbm, steps_hbm, comps_hbm, w_ref,
    xout_ref, w2_ref, shift_ref, gram_ref, target_ref,
    normed, xsend, xrecv, off, ids, tops, sums, hits, stat, stats, dsend, drecv,
    gsend, grecv,
    hidden_ref, gain_ref, bias_ref, ids_ref, steps_ref, comps_ref, in_sem,
    send_sem, recv_sem, out_sem, ssend, srecv, dssem, drsem, gssem, grsem,
):
    owners, shards, tokens, width, tile, chunks = sizes
    slab = tokens // owners
    rows = owners * slab
    kinds = COMPONENTS
    me = lax.axis_index("ckpt")
    mine = lax.axis_index("vocab")
    step = pl.program_id(0)
    groups = tile // LANES
    my_rows = pl.ds(pl.multiple_of(me * slab, slab), slab)

    def peer(r):
        return lax.rem(me + r, owners)

    def side(r):
        return lax.rem(mine + r, shards)

    @pl.when(step == 0)
    def _():
        loads = []
        for i, (src, dst) in enumerate((
            (hidden_hbm, hidden_ref), (gain_hbm, gain_ref), (bias_hbm, bias_ref),
            (ids_hbm, ids_ref), (steps_hbm, steps_ref), (comps_hbm, comps_ref),
        )):
            load = pltpu.make_async_copy(src, dst, in_sem.at[i])
            load.start()
            loads.append(load)
        barrier = pltpu.get_barrier_semaphore()
        for q in range(shards):
            for r in range(owners):
                if q or r:
                    pl.semaphore_signal(
                        barrier, inc=1, device_id=(peer(r), side(q)), device_id_type=MESH
                    )
        for load in loads:
            load.wait()
        floats = hidden_ref[...].astype(jnp.float32)
        centre = jnp.mean(floats, axis=1, keepdims=True)
        spread = jnp.mean((floats - centre) ** 2, axis=1, keepdims=True)
        normed[...] = (
            (floats - centre) / jnp.sqrt(spread + 1e-05) * gain_ref[...] + bias_ref[...]
        ).astype(jnp.bfloat16)
        wide = jnp.broadcast_to(ids_ref[...].astype(jnp.float32), (LANES, tokens))
        ids[...] = jnp.transpose(wide).astype(jnp.int32)
        tops[...] = jnp.full_like(tops, LOW)
        sums[...] = jnp.zeros_like(sums)
        hits[...] = jnp.zeros_like(hits)

    logits = lax.dot_general(normed[...], w_ref[...], NT, preferred_element_type=jnp.float32)
    first = step * tile
    lane = lax.broadcasted_iota(jnp.int32, (tokens, LANES), 1)

    @pl.when(step == 0)
    def _():
        total = logits[:, :LANES]
        for g in range(1, groups):
            total = total + logits[:, g * LANES:(g + 1) * LANES]
        off[...] = jnp.broadcast_to(
            jnp.sum(total, axis=1, keepdims=True) * (1.0 / tile), off.shape
        )

    shift = off[...]
    for g in range(groups):
        part = logits[:, g * LANES:(g + 1) * LANES]
        inside = (first + g * LANES + lane) < width
        at = pl.multiple_of(first + g * LANES, LANES)
        xsend[:, pl.ds(at, LANES)] = jnp.where(inside, part - shift, 0.0).astype(jnp.bfloat16)

    @pl.when(step == 0)
    def _():
        barrier = pltpu.get_barrier_semaphore()
        pl.semaphore_wait(barrier, owners * shards - 1)

    def columns(j):
        return pl.ds(pl.multiple_of(j * tile, LANES), tile)

    for r in range(1, owners):
        to = peer(r)
        pltpu.make_async_remote_copy(
            src_ref=xsend.at[pl.ds(pl.multiple_of(to * slab, slab), slab), columns(step)],
            dst_ref=xrecv.at[my_rows, columns(step)],
            send_sem=send_sem.at[r],
            recv_sem=recv_sem.at[step],
            device_id=(to, mine),
            device_id_type=MESH,
        ).start()
    pltpu.make_async_copy(
        xsend.at[my_rows, columns(step)], xrecv.at[my_rows, columns(step)], recv_sem.at[step]
    ).start()

    old_top = tops[...]
    new_top = old_top
    parts = []
    for g in range(groups):
        part = logits[:, g * LANES:(g + 1) * LANES]
        inside = (first + g * LANES + lane) < width
        part = jnp.where(inside, part, LOW)
        parts.append(part)
        new_top = jnp.maximum(new_top, part)
    acc = sums[...] * jnp.exp(old_top - new_top)
    hit = hits[...]
    start = mine * width + first
    wanted = ids[...] - start
    for g in range(groups):
        acc = acc + jnp.exp(parts[g] - new_top)
        col = g * LANES + lane
        hit = hit + jnp.where((col == wanted) & ((first + col) < width), parts[g], 0.0)
    tops[...] = new_top
    sums[...] = acc
    hits[...] = hit

    @pl.when(step == chunks - 1)
    def _():
        top = jnp.max(tops[...], axis=1, keepdims=True)
        total = jnp.sum(sums[...] * jnp.exp(tops[...] - top), axis=1, keepdims=True)
        picked = jnp.sum(hits[...], axis=1, keepdims=True)
        stat[...] = jnp.where(lane == 0, top, jnp.where(lane == 1, total, picked))
        sent = []
        for r in range(1, shards):
            copy = pltpu.make_async_remote_copy(
                src_ref=stat,
                dst_ref=stats.at[r - 1],
                send_sem=ssend.at[r - 1],
                recv_sem=srecv.at[r - 1],
                device_id=(me, side(r)),
                device_id_type=MESH,
            )
            copy.start()
            sent.append(copy)
        for copy in sent:
            copy.wait()
        best = top
        for r in range(shards - 1):
            best = jnp.maximum(best, stats[r][:, 0:1])
        total = total * jnp.exp(top - best)
        for r in range(shards - 1):
            total = total + stats[r][:, 1:2] * jnp.exp(stats[r][:, 0:1] - best)
            picked = picked + stats[r][:, 2:3]
        lse = best + jnp.log(total)
        dsend[...] = jnp.broadcast_to(off[:, 0:1] - lse, dsend.shape)
        dcopies = []
        for r in range(1, owners):
            to = peer(r)
            copy = pltpu.make_async_remote_copy(
                src_ref=dsend.at[pl.ds(pl.multiple_of(to * slab, slab), slab), :],
                dst_ref=drecv.at[my_rows, :],
                send_sem=dssem.at[0],
                recv_sem=drsem.at[0],
                device_id=(to, mine),
                device_id_type=MESH,
            )
            copy.start()
        pltpu.make_async_copy(dsend.at[my_rows, :], drecv.at[my_rows, :], drsem.at[0]).start()
        target_ref[...] = jnp.transpose(
            jnp.broadcast_to(picked - lse, (tokens, LANES))
        )[0:1, :]

        flats = max(owners * owners, LANES)

        def iota(shape, axis):
            return lax.broadcasted_iota(jnp.int32, shape, axis)

        slot = mine * owners + me
        flat_lane = iota((owners, flats), 1)
        flat_own = flat_lane // owners == iota((owners, flats), 0)
        flat_diag = iota((1, flats), 1) // owners == iota((1, flats), 1) % owners
        to_flat = (iota((rows, flats), 0) // slab == iota((rows, flats), 1) % owners).astype(
            jnp.float32
        )
        from_flat = (iota((flats, rows), 0) // owners == iota((flats, rows), 1) // slab).astype(
            jnp.float32
        )
        flat_pick = (iota((flats, LANES), 0) % owners == iota((flats, LANES), 1)).astype(
            jnp.float32
        ) - 1.0 / owners
        row_k = iota((kinds * slab, flats), 0) // slab
        at_steps = spread_steps(steps_ref, (kinds * slab, flats))
        basis = jnp.cos(jnp.pi * (row_k + 1).astype(jnp.float32) * at_steps / 143000.0)
        flat_basis = basis - jnp.mean(basis, axis=1, keepdims=True)
        row_r = iota((kinds * slab, rows), 0)
        same = (row_r % slab) == (iota((kinds * slab, rows), 1) % slab)
        keep = same & (row_r // slab < comps_ref[0])
        ones = jnp.ones((tile, LANES), jnp.bfloat16)

        def absorb(j, carry):
            products, totals = carry
            block = xrecv.at[:, columns(j)]
            pltpu.make_async_copy(block, block, recv_sem.at[j]).wait()
            pltpu.make_async_copy(block, xout_ref.at[:, columns(j)], out_sem.at[0]).start()
            x = block[...]
            products = products + lax.dot_general(x, x, NT, preferred_element_type=jnp.float32)
            totals = totals + jnp.dot(x, ones, preferred_element_type=jnp.float32)
            return products, totals

        products, totals = lax.fori_loop(
            0, chunks, absorb,
            (jnp.zeros((rows, rows), jnp.float32), jnp.zeros((rows, LANES), jnp.float32)),
        )
        pltpu.make_async_copy(drecv, drecv, drsem.at[0]).wait()
        d = drecv[...].reshape(owners, slab, LANES)
        d = (d - jnp.mean(d, axis=0, keepdims=True)).reshape(rows, LANES)
        d_row = jnp.transpose(d)[0:1, :]
        lane_r = lax.broadcasted_iota(jnp.int32, (rows, LANES), 1)
        left = jnp.where(lane_r == 0, totals, jnp.where(lane_r == 1, d, 0.0))
        right = jnp.where(
            lane_r == 0, d, jnp.where(lane_r == 1, totals + float(width) * d, 0.0)
        )
        products = products + lax.dot_general(
            left, right, NT, precision=HIGH, preferred_element_type=jnp.float32
        )
        matched = (
            lax.broadcasted_iota(jnp.int32, (rows, rows), 0) % slab
            == lax.broadcasted_iota(jnp.int32, (rows, rows), 1) % slab
        )
        partial = jnp.sum(
            jnp.where(matched, products, 0.0).reshape(owners, slab, rows), axis=1
        )
        partial = partial - jnp.mean(partial, axis=0, keepdims=True)
        spreadout = jnp.dot(partial, to_flat, precision=HIGH, preferred_element_type=jnp.float32)
        gsend[...] = jnp.sum(jnp.where(flat_own, spreadout, 0.0), axis=0, keepdims=True)
        for q in range(shards):
            for r in range(owners):
                if q or r:
                    pltpu.make_async_remote_copy(
                        src_ref=gsend,
                        dst_ref=grecv.at[slot],
                        send_sem=gssem.at[0],
                        recv_sem=grsem.at[0],
                        device_id=(peer(r), side(q)),
                        device_id_type=MESH,
                    ).start()
        pltpu.make_async_copy(gsend, grecv.at[slot], grsem.at[0]).start()
        pltpu.make_async_copy(grecv, grecv, grsem.at[0]).wait()
        flat = jnp.sum(grecv[...], axis=0) * (1.0 / (tokens * width * shards))
        trace = jnp.sum(jnp.where(flat_diag, flat, 0.0), axis=1, keepdims=True)
        mixed = jnp.dot(
            flat_basis * flat, from_flat, precision=HIGH, preferred_element_type=jnp.float32
        )
        mixed = jnp.where(keep, mixed / (trace * (1.0 / owners) + 1e-06) * (1.0 / owners), 0.0)
        high = mixed.astype(jnp.bfloat16)
        half = mixed.shape[0]
        w2_ref[0:half, :] = high
        w2_ref[half:, :] = (mixed - high.astype(jnp.float32)).astype(jnp.bfloat16)
        shift_ref[...] = jnp.broadcast_to(
            jnp.sum(mixed * d_row, axis=1, keepdims=True), shift_ref.shape
        )
        gram_ref[...] = jnp.dot(
            jnp.where(flat_own, flat, 0.0), flat_pick, precision=HIGH,
            preferred_element_type=jnp.float32,
        )[:, :owners]

        for r in range(1, owners):
            strip = xsend.at[my_rows, :]
            pltpu.make_async_copy(strip, strip, send_sem.at[r]).wait()
        others = pl.ds(0, rows - slab)
        pltpu.make_async_copy(dsend.at[others, :], dsend.at[others, :], dssem.at[0]).wait()
        less = pl.ds(0, owners * shards - 1)
        pltpu.make_async_copy(grecv.at[less], grecv.at[less], gssem.at[0]).wait()
        pltpu.make_async_copy(xrecv, xout_ref, out_sem.at[0]).wait()


def mix_kernel(across, x_ref, w2_ref, shift_ref, gram_in, target_in, out_ref, gram_ref, target_ref):
    start = pl.multiple_of(pl.program_id(0) * across, LANES)
    x = x_ref[:, pl.ds(start, across)]
    both = jnp.dot(w2_ref[...], x, preferred_element_type=jnp.float32)
    half = out_ref.shape[0]
    out_ref[...] = (both[:half] + both[half:] + shift_ref[:, 0:1]).astype(jnp.bfloat16)
    gram_ref[...] = gram_in[...]
    target_ref[...] = target_in[...]


def per_device(owners, shards, hidden_rows, norm_gain, norm_bias, unembed, target_ids, ckpt_steps, components):
    tokens, depth = hidden_rows.shape[1:]
    width = unembed.shape[2]
    slab = tokens // owners
    rows = owners * slab
    out_rows = COMPONENTS * slab
    tile, chunks = split_tiles(width)
    padded = tile * chunks
    sizes = (owners, shards, tokens, width, tile, chunks)
    f32, bf16 = jnp.float32, jnp.bfloat16
    limit = 67043328 - min(depth * width * 2 - (1 << 20), 16 << 20)
    vmem = pl.BlockSpec(memory_space=pltpu.VMEM)
    hbm = pl.BlockSpec(memory_space=pltpu.HBM)
    dma = pltpu.SemaphoreType.DMA

    x, w2, shift, gram, target = pl.pallas_call(
        functools.partial(gather_kernel, sizes),
        grid=(chunks,),
        in_specs=[
            hbm, hbm, hbm, hbm, hbm, hbm,
            pl.BlockSpec((tile, depth), lambda j: (j, 0)),
        ],
        out_specs=[pl.BlockSpec(memory_space=pl.ANY), vmem, vmem, vmem, vmem],
        out_shape=[
            jax.ShapeDtypeStruct((rows, padded), bf16),
            jax.ShapeDtypeStruct((2 * out_rows, rows), bf16),
            jax.ShapeDtypeStruct((out_rows, LANES), f32),
            jax.ShapeDtypeStruct((owners, owners), f32),
            jax.ShapeDtypeStruct((1, tokens), f32),
        ],
        scratch_shapes=[
            pltpu.VMEM((tokens, depth), bf16),
            pltpu.VMEM((tokens, padded), bf16),
            pltpu.VMEM((rows, padded), bf16),
            pltpu.VMEM((tokens, LANES), f32),
            pltpu.VMEM((tokens, LANES), jnp.int32),
            pltpu.VMEM((tokens, LANES), f32),
            pltpu.VMEM((tokens, LANES), f32),
            pltpu.VMEM((tokens, LANES), f32),
            pltpu.VMEM((tokens, LANES), f32),
            pltpu.VMEM((shards - 1, tokens, LANES), f32),
            pltpu.VMEM((tokens, LANES), f32),
            pltpu.VMEM((rows, LANES), f32),
            pltpu.VMEM((1, max(owners * owners, LANES)), f32),
            pltpu.VMEM((owners * shards, 1, max(owners * owners, LANES)), f32),
            pltpu.VMEM((tokens, depth), bf16),
            pltpu.VMEM((1, depth), f32),
            pltpu.VMEM((1, depth), f32),
            pltpu.VMEM((1, tokens), jnp.int32),
            pltpu.SMEM((owners,), jnp.int32),
            pltpu.SMEM((1,), jnp.int32),
            dma((6,)),
            dma((owners,)), dma((chunks,)), dma((1,)),
            dma((shards - 1,)), dma((shards - 1,)),
            dma((1,)), dma((1,)), dma((1,)), dma((1,)),
        ],
        compiler_params=pltpu.CompilerParams(
            collective_id=0, has_side_effects=True, vmem_limit_bytes=limit,
            dimension_semantics=("arbitrary",),
        ),
    )(*(
        pltpu.with_memory_space_constraint(a, pltpu.HBM) for a in (
            hidden_rows[0], norm_gain, norm_bias, target_ids.reshape(1, tokens), ckpt_steps,
        )
    ), components, unembed[0].T)

    across = -(-(padded // LANES) // 3) * LANES
    out, gram, target = pl.pallas_call(
        functools.partial(mix_kernel, across),
        grid=(padded // across,),
        in_specs=[vmem, vmem, vmem, vmem, vmem],
        out_specs=[pl.BlockSpec((out_rows, across), lambda j: (0, j)), vmem, vmem],
        out_shape=[
            jax.ShapeDtypeStruct((out_rows, width), bf16),
            jax.ShapeDtypeStruct((owners, owners), f32),
            jax.ShapeDtypeStruct((1, tokens), f32),
        ],
        compiler_params=pltpu.CompilerParams(
            dimension_semantics=("arbitrary",),
            vmem_limit_bytes=rows * padded * 2 + 12 * out_rows * across + (6 << 20),
        ),
    )(x, w2, shift, gram, target)
    return out.reshape(COMPONENTS, slab, width), gram, target


def solution(mesh):
    return jax.shard_map(
        functools.partial(per_device, mesh.shape["ckpt"], mesh.shape["vocab"]),
        mesh=mesh,
        in_specs=(
            P("ckpt", None, None),
            P("ckpt", None),
            P("ckpt", None),
            P("ckpt", None, "vocab"),
            P(),
            P(),
            P(),
        ),
        out_specs=(P(None, "ckpt", "vocab"), P(), P("ckpt", None)),
        check_vma=False,
    )
```

profile of v0, /device:TPU:0, one launch (start us, length us, event | category | flops | bytes accessed | tf_op | source)
XLA Modules:
  0.0 55.4 jit_solution(17574855789525596128)
XLA Ops:
  1.3 50.7 %shard_map.94 = (bf16[128,12672]{1,0:T(8,128)(2,1)S(1)}, bf16[256,128]{1,0:T(8,128)(2,1)S(1)}, f32[128,128]{1,0:T(8,128)S(1)}, f32[8,8]{1,0:T(8,128)S(1)}, f32[1,128]{1,0:T(1,128)S(1)}) custom-call(bf16[128,768]{1,0:T(8,128)(2,1)} %bitcast.7, f32[1,768]{1,0:T(1,128)} %gain_hbm.1, f32[1,768]{1,0:T(1,128)} %bias_hbm.1, s32[1,128]{1,0:T(1,128)} %bitcast.8, ...), custom_call_target="tpu_custom_call" | custom-call | tf_op jit(solution)/shard_map/pallas_call | solution.py:330
  52.0 3.4 %shard_map.95 = (bf16[128,12576]{1,0:T(8,128)(2,1)}, f32[8,8]{1,0:T(8,128)}, f32[1,128]{1,0:T(1,128)}) custom-call(bf16[128,12672]{1,0:T(8,128)(2,1)S(1)} %get-tuple-element.11.x_ref, bf16[256,128]{1,0:T(8,128)(2,1)S(1)} %get-tuple-element.12.w2_ref, f32[128,128]{1,0:T(8,128)S(1)} %get-tuple-element.13.shift_ref, f32[8,8]{1,0:T(8,128)S(1)} %get-tuple-element.14.gram_in, ...), custom_call_target="tpu_custom_call" | custom-call | tf_op jit(solution)/shard_map/pallas_call | solution.py:382
where the time goes:
time: 55.8 us; the launch traced here: 55.4 us
  Pallas kernels  54.1 us (97%)
  between operations  1.29 us (2%)
    pallas_call x1, Pallas kernels, per_device(): pl.pallas_call(functools.partial(gather_kernel, sizes), grid=(chunks,), i...  50.7 us
    pallas_call x1, Pallas kernels, per_device(): pl.pallas_call(functools.partial(mix_kernel, across), grid=(padded // acr...  3.43 us

commit v1 on v0

v1 whole, which is shorter than its diff:
```python
import functools

import jax
import jax.numpy as jnp
from jax import lax
from jax.experimental import pallas as pl
from jax.experimental.pallas import tpu as pltpu
from jax.sharding import PartitionSpec as P

COMPONENTS = 8
LANES = 128
MESH = pl.DeviceIdType.MESH
LOW = -1e30
NT = (((1,), (1,)), ((), ()))
RING = 4
STEPS = 2
HOLD = 4


def split_tiles(width):
    tiles = -(-width // LANES)
    best = tiles
    for per in range(1, tiles + 1):
        if tiles % per == 0 and per >= 6:
            best = per
            break
    return best * LANES, tiles // best


def spread_steps(steps_ref, shape):
    lane_owner = lax.broadcasted_iota(jnp.int32, shape, 1) % steps_ref.shape[0]
    out = jnp.zeros(shape, jnp.float32)
    for c in range(steps_ref.shape[0]):
        out = jnp.where(lane_owner == c, steps_ref[c].astype(jnp.float32), out)
    return out


def halves(value):
    high = value.astype(jnp.bfloat16)
    return high, (value - high.astype(jnp.float32)).astype(jnp.bfloat16)


def select_sum(value, table):
    count = value.shape[0]
    both = jnp.dot(
        jnp.concatenate(halves(value), axis=0), table, preferred_element_type=jnp.float32
    )
    return both[:count] + both[count:]


def gather_kernel(
    sizes,
    hidden_hbm, gain_hbm, bias_hbm, ids_hbm, steps_hbm, comps_hbm, w_hbm,
    xout_ref, w2_ref, gexp_ref, target_ref,
    normed, wbuf, xsend, xrecv, off, ids, tops, sums, hits, stat, stats, dsend, drecv,
    gsend, grecv, basis, to_flat, from_flat,
    hidden_ref, gain_ref, bias_ref, ids_ref, steps_ref, comps_ref, in_sem, wsem,
    send_sem, recv_sem, ssend, srecv, dssem, drsem, gssem, grsem, out_sem,
):
    owners, shards, tokens, width, tile, chunks = sizes
    slab = tokens // owners
    rows = owners * slab
    kinds = COMPONENTS
    ring = wbuf.shape[0]
    cut = (tile // LANES // 3) * LANES
    flats = gsend.shape[1]
    me = lax.axis_index("ckpt")
    mine = lax.axis_index("vocab")
    my_rows = pl.ds(pl.multiple_of(me * slab, slab), slab)
    last = chunks - 1
    last_rows = width - last * tile

    def peer(r):
        return lax.rem(me + r, owners)

    def side(r):
        return lax.rem(mine + r, shards)

    def iota(shape, axis):
        return lax.broadcasted_iota(jnp.int32, shape, axis)

    def fetch(j, slot, begin=0, count=None, sem=None):
        count = tile if count is None else count
        start = j * tile + begin
        return pltpu.make_async_copy(
            w_hbm.at[pl.ds(start if isinstance(start, int) else pl.multiple_of(start, LANES), count), :],
            wbuf.at[slot, pl.ds(begin, count), :],
            wsem.at[slot if sem is None else sem],
        )

    loads = []
    for i, (src, dst) in enumerate((
        (hidden_hbm, hidden_ref), (gain_hbm, gain_ref), (bias_hbm, bias_ref),
        (ids_hbm, ids_ref), (steps_hbm, steps_ref), (comps_hbm, comps_ref),
    )):
        loads.append(pltpu.make_async_copy(src, dst, in_sem.at[i]))
    for load in loads[:3]:
        load.start()
    fetch(0, 0, 0, cut).start()
    barrier = pltpu.get_barrier_semaphore()
    for q in range(shards - 1, -1, -1):
        for r in range(owners - 1, -1, -1):
            if q or r:
                pl.semaphore_signal(
                    barrier, inc=1, device_id=(peer(r), side(q)), device_id_type=MESH
                )
    fetch(0, 0, cut, tile - cut, ring).start()
    for load in loads[3:]:
        load.start()
    for j in range(1, ring):
        if j == last:
            fetch(j, j % ring, 0, last_rows).start()
        elif j < last:
            fetch(j, j % ring).start()
    for load in loads[:3]:
        load.wait()
    floats = hidden_ref[...].astype(jnp.float32)
    centre = jnp.mean(floats, axis=1, keepdims=True)
    spread = jnp.mean((floats - centre) ** 2, axis=1, keepdims=True)
    normed[...] = (
        (floats - centre) / jnp.sqrt(spread + 1e-05) * gain_ref[...] + bias_ref[...]
    ).astype(jnp.bfloat16)
    lane = iota((tokens, LANES), 1)

    def columns(start, count):
        return pl.ds(start if isinstance(start, int) else pl.multiple_of(start, LANES), count)

    def logits_of(slot, begin, count):
        return lax.dot_general(
            normed[...], wbuf[slot, pl.ds(begin, count), :], NT,
            preferred_element_type=jnp.float32,
        )

    def split_parts(logits, start, edge):
        parts = []
        for g in range(logits.shape[1] // LANES):
            part = logits[:, g * LANES:(g + 1) * LANES]
            inside = None
            if edge and start + (g + 1) * LANES > width:
                inside = (start + g * LANES + lane) < width
            parts.append((part, inside))
        return parts

    def store(parts, start):
        shift = off[...]
        for g, (part, inside) in enumerate(parts):
            value = part - shift
            if inside is not None:
                value = jnp.where(inside, value, 0.0)
            xsend[:, columns(start + g * LANES, LANES)] = value.astype(jnp.bfloat16)

    def send(start, count, piece):
        for r in range(1, owners):
            to = peer(r)
            pltpu.make_async_remote_copy(
                src_ref=xsend.at[
                    pl.ds(pl.multiple_of(to * slab, slab), slab), columns(start, count)
                ],
                dst_ref=xrecv.at[my_rows, columns(start, count)],
                send_sem=send_sem.at[r],
                recv_sem=recv_sem.at[piece],
                device_id=(to, mine),
                device_id_type=MESH,
            ).start()
        pltpu.make_async_copy(
            xsend.at[my_rows, columns(start, count)],
            xrecv.at[my_rows, columns(start, count)],
            recv_sem.at[piece],
        ).start()

    def gather_stats(parts, start):
        old_top = tops[...]
        new_top = old_top
        kept = []
        for part, inside in parts:
            if inside is not None:
                part = jnp.where(inside, part, LOW)
            kept.append(part)
            new_top = jnp.maximum(new_top, part)
        acc = sums[...] * jnp.exp(old_top - new_top)
        hit = hits[...]
        wanted = ids[...] - (mine * width + start)
        for g, (part, inside) in enumerate(parts):
            acc = acc + jnp.exp(kept[g] - new_top)
            match = (g * LANES + lane) == wanted
            if inside is not None:
                match = match & inside
            hit = hit + jnp.where(match, part, 0.0)
        tops[...] = new_top
        sums[...] = acc
        hits[...] = hit

    fetch(0, 0, 0, cut).wait()
    logits = logits_of(0, 0, cut)
    total = logits[:, :LANES]
    for g in range(1, cut // LANES):
        total = total + logits[:, g * LANES:(g + 1) * LANES]
    off[...] = jnp.broadcast_to(
        jnp.sum(total, axis=1, keepdims=True) * (1.0 / cut), off.shape
    )
    parts = split_parts(logits, 0, False)
    store(parts, 0)
    pl.semaphore_wait(barrier, owners * shards - 1)
    send(0, cut, 0)
    for load in loads[3:]:
        load.wait()
    wide = jnp.broadcast_to(ids_ref[...].astype(jnp.float32), (LANES, tokens))
    ids[...] = jnp.transpose(wide).astype(jnp.int32)
    tops[...] = jnp.full_like(tops, LOW)
    sums[...] = jnp.zeros_like(sums)
    hits[...] = jnp.zeros_like(hits)

    fetch(0, 0, cut, tile - cut, ring).wait()
    more = logits_of(0, cut, tile - cut)
    more_parts = split_parts(more, cut, False)
    store(more_parts, cut)
    send(cut, tile - cut, 1)
    gather_stats(parts, 0)
    gather_stats(more_parts, cut)
    if ring == last:
        fetch(last, 0, 0, last_rows).start()
    elif ring < last:
        fetch(ring, 0).start()

    held = max(1, last - HOLD)

    def middle(j, carry):
        slot = lax.rem(j, ring)
        start = j * tile
        fetch(j, slot).wait()
        chunk_parts = split_parts(logits_of(slot, 0, tile), start, False)
        store(chunk_parts, start)

        @pl.when(j < held)
        def _():
            send(start, tile, j + 1)

        gather_stats(chunk_parts, start)

        @pl.when(j + ring < last)
        def _():
            fetch(j + ring, slot).start()

        @pl.when(j + ring == last)
        def _():
            fetch(last, slot, 0, last_rows).start()

        return carry

    lax.fori_loop(1, last, middle, 0)
    tail_at = last * tile
    fetch(last, last % ring, 0, last_rows).wait()
    tail_parts = split_parts(logits_of(last % ring, 0, tile), tail_at, True)
    store(tail_parts, tail_at)
    gather_stats(tail_parts, tail_at)

    top = jnp.max(tops[...], axis=1, keepdims=True)
    total = jnp.sum(sums[...] * jnp.exp(tops[...] - top), axis=1, keepdims=True)
    picked = jnp.sum(hits[...], axis=1, keepdims=True)
    stat[...] = jnp.where(lane == 0, top, jnp.where(lane == 1, total, picked))
    sent = []
    for r in range(1, shards):
        copy = pltpu.make_async_remote_copy(
            src_ref=stat,
            dst_ref=stats.at[r - 1],
            send_sem=ssend.at[r - 1],
            recv_sem=srecv.at[r - 1],
            device_id=(me, side(r)),
            device_id_type=MESH,
        )
        copy.start()
        sent.append(copy)

    to_flat[...] = (iota((rows, flats), 0) // slab == iota((rows, flats), 1) % owners).astype(
        jnp.bfloat16
    )
    from_flat[...] = (
        iota((flats, rows), 0) % owners == iota((flats, rows), 1) // slab
    ).astype(jnp.bfloat16)
    at_steps = spread_steps(steps_ref, (kinds, LANES))
    cosines = jnp.cos(
        jnp.pi * (iota((kinds, LANES), 0) + 1).astype(jnp.float32) * at_steps / 143000.0
    )
    level = jnp.sum(
        jnp.where(iota((kinds, LANES), 1) < owners, cosines, 0.0), axis=1, keepdims=True
    ) * (1.0 / owners)
    for d in range(owners):
        basis[d] = jnp.broadcast_to(cosines[:, d:d + 1] - level, (kinds, rows))

    for copy in sent:
        copy.wait()
    best = top
    for r in range(shards - 1):
        best = jnp.maximum(best, stats[r][:, 0:1])
    total = total * jnp.exp(top - best)
    for r in range(shards - 1):
        total = total + stats[r][:, 1:2] * jnp.exp(stats[r][:, 0:1] - best)
        picked = picked + stats[r][:, 2:3]
    lse = best + jnp.log(total)
    dsend[...] = jnp.broadcast_to(off[:, 0:1] - lse, dsend.shape)
    for r in range(1, owners):
        to = peer(r)
        pltpu.make_async_remote_copy(
            src_ref=dsend.at[pl.ds(pl.multiple_of(to * slab, slab), slab), :],
            dst_ref=drecv.at[my_rows, :],
            send_sem=dssem.at[0],
            recv_sem=drsem.at[0],
            device_id=(to, mine),
            device_id_type=MESH,
        ).start()
    pltpu.make_async_copy(dsend.at[my_rows, :], drecv.at[my_rows, :], drsem.at[0]).start()

    def late(j, carry):
        send(j * tile, tile, j + 1)
        return carry

    lax.fori_loop(held, last, late, 0)
    send(tail_at, tile - cut, chunks)
    send(tail_at + tile - cut, cut, chunks + 1)
    target_ref[...] = jnp.transpose(
        jnp.broadcast_to(picked - lse, (tokens, LANES))
    )[0:1, :]

    pltpu.make_async_copy(drecv, drecv, drsem.at[0]).wait()
    d = drecv[...].reshape(owners, slab, LANES)
    d = d - jnp.mean(d, axis=0, keepdims=True)
    drecv[...] = d.reshape(rows, LANES)

    def absorb(start, count, piece, products, edge=False):
        block = xrecv.at[:, columns(start, count)]
        pltpu.make_async_copy(block, block, recv_sem.at[piece]).wait()
        level = drecv[...].reshape(owners, slab, LANES)
        for g in range(count // LANES):
            at = columns(start + g * LANES, LANES)
            x = xrecv[:, at].astype(jnp.float32).reshape(owners, slab, LANES)
            x = x - jnp.mean(x, axis=0, keepdims=True) + level
            if edge and start + (g + 1) * LANES > width:
                x = jnp.where(start + g * LANES + iota(x.shape, 2) < width, x, 0.0)
            xrecv[:, at] = x.reshape(rows, LANES).astype(jnp.bfloat16)
        kept = xrecv[:, columns(start, count)]
        pltpu.make_async_copy(block, xout_ref.at[:, columns(start, count)], out_sem.at[0]).start()
        return products + lax.dot_general(kept, kept, NT, preferred_element_type=jnp.float32)

    products = absorb(0, cut, 0, jnp.zeros((rows, rows), jnp.float32))
    products = absorb(cut, tile - cut, 1, products)
    products = lax.fori_loop(
        1, last, lambda j, p: absorb(j * tile, tile, j + 1, p), products
    )
    products = absorb(tail_at, tile - cut, chunks, products, True)
    products = absorb(tail_at + tile - cut, cut, chunks + 1, products, True)

    matched = iota((rows, rows), 0) % slab == iota((rows, rows), 1) % slab
    partial = jnp.sum(
        jnp.where(matched, products, 0.0).reshape(owners, slab, rows), axis=1
    )
    flat_own = iota((owners, flats), 1) // owners == iota((owners, flats), 0)
    gsend[...] = jnp.sum(
        jnp.where(flat_own, select_sum(partial, to_flat[...]), 0.0), axis=0, keepdims=True
    )
    slot = mine * owners + me
    for q in range(shards - 1, -1, -1):
        for r in range(owners - 1, -1, -1):
            if q or r:
                pltpu.make_async_remote_copy(
                    src_ref=gsend,
                    dst_ref=grecv.at[slot],
                    send_sem=gssem.at[0],
                    recv_sem=grsem.at[0],
                    device_id=(peer(r), side(q)),
                    device_id_type=MESH,
                ).start()
    pltpu.make_async_copy(gsend, grecv.at[slot], grsem.at[0]).start()
    for r in range(1, owners):
        strip = xsend.at[my_rows, :]
        pltpu.make_async_copy(strip, strip, send_sem.at[r]).wait()
    others = pl.ds(0, rows - slab)
    pltpu.make_async_copy(dsend.at[others, :], dsend.at[others, :], dssem.at[0]).wait()
    row_k = iota((kinds, slab, rows), 0)
    keep = (iota((kinds, slab, rows), 2) % slab == iota((kinds, slab, rows), 1)) & (
        row_k < comps_ref[0]
    )
    flat_diag = iota((1, flats), 1) // owners == iota((1, flats), 1) % owners

    pltpu.make_async_copy(grecv, grecv, grsem.at[0]).wait()
    flat = jnp.sum(grecv[...], axis=0) * (1.0 / (tokens * width * shards))
    trace = jnp.sum(jnp.where(flat_diag, flat, 0.0), axis=1, keepdims=True)
    gexp = select_sum(
        jnp.where(flat_own, jnp.broadcast_to(flat, flat_own.shape), 0.0), from_flat[...]
    )
    mixed = basis[0] * gexp[0:1, :]
    for d in range(1, owners):
        mixed = mixed + basis[d] * gexp[d:d + 1, :]
    mixed = mixed * (1.0 / (trace * (1.0 / owners) + 1e-06) * (1.0 / owners))
    spreadout = jnp.where(
        keep, jnp.broadcast_to(mixed.reshape(kinds, 1, rows), keep.shape), 0.0
    ).reshape(kinds * slab, rows)
    high, low = halves(spreadout)
    w2_ref[:, 0:rows] = high
    w2_ref[:, rows:] = low
    gexp_ref[...] = gexp
    pltpu.make_async_copy(xrecv, xout_ref.at[:, columns(0, tile * chunks)], out_sem.at[0]).wait()
    less = pl.ds(0, owners * shards - 1)
    pltpu.make_async_copy(grecv.at[less], grecv.at[less], gssem.at[0]).wait()


def mix_kernel(across, x_ref, w2_ref, gexp_ref, target_in, out_ref, gram_ref, target_ref):
    start = pl.multiple_of(pl.program_id(0) * across, LANES)
    x = x_ref[:, pl.ds(start, across)]
    out_ref[...] = jnp.dot(
        w2_ref[...], jnp.concatenate([x, x], axis=0), preferred_element_type=jnp.float32
    ).astype(jnp.bfloat16)

    @pl.when(pl.program_id(0) == pl.num_programs(0) - 1)
    def _():
        owners, rows = gexp_ref.shape
        pick = (
            lax.broadcasted_iota(jnp.int32, (rows, LANES), 0)
            == lax.broadcasted_iota(jnp.int32, (rows, LANES), 1) * (rows // owners)
        ).astype(jnp.float32)
        gram_ref[...] = jnp.dot(
            gexp_ref[...], pick, precision=lax.Precision.HIGHEST,
            preferred_element_type=jnp.float32,
        )[:, :owners]
        target_ref[...] = target_in[...]


def per_device(owners, shards, hidden_rows, norm_gain, norm_bias, unembed, target_ids, ckpt_steps, components):
    tokens, depth = hidden_rows.shape[1:]
    width = unembed.shape[2]
    slab = tokens // owners
    rows = owners * slab
    out_rows = COMPONENTS * slab
    tile, chunks = split_tiles(width)
    padded = tile * chunks
    across = -(-(padded // LANES) // STEPS) * LANES
    flats = max(owners * owners, LANES)
    ring = min(RING, chunks)
    sizes = (owners, shards, tokens, width, tile, chunks)
    f32, bf16 = jnp.float32, jnp.bfloat16
    vmem = pl.BlockSpec(memory_space=pltpu.VMEM)
    hbm = pl.BlockSpec(memory_space=pltpu.HBM)
    dma = pltpu.SemaphoreType.DMA
    limit = 67043328 - min(depth * width * 2 - (1 << 20), 16 << 20)

    def far(a):
        return pltpu.with_memory_space_constraint(a, pltpu.HBM)

    x, w2, gexp, target = pl.pallas_call(
        functools.partial(gather_kernel, sizes),
        in_specs=[hbm] * 7,
        out_specs=[pl.BlockSpec(memory_space=pl.ANY), vmem, vmem, vmem],
        out_shape=[
            jax.ShapeDtypeStruct((rows, across * STEPS), bf16),
            jax.ShapeDtypeStruct((out_rows, 2 * rows), bf16),
            jax.ShapeDtypeStruct((owners, rows), f32),
            jax.ShapeDtypeStruct((1, tokens), f32),
        ],
        scratch_shapes=[
            pltpu.VMEM((tokens, depth), bf16),
            pltpu.VMEM((ring, tile, depth), bf16),
            pltpu.VMEM((tokens, padded), bf16),
            pltpu.VMEM((rows, padded), bf16),
            pltpu.VMEM((tokens, LANES), f32),
            pltpu.VMEM((tokens, LANES), jnp.int32),
            pltpu.VMEM((tokens, LANES), f32),
            pltpu.VMEM((tokens, LANES), f32),
            pltpu.VMEM((tokens, LANES), f32),
            pltpu.VMEM((tokens, LANES), f32),
            pltpu.VMEM((shards - 1, tokens, LANES), f32),
            pltpu.VMEM((tokens, LANES), f32),
            pltpu.VMEM((rows, LANES), f32),
            pltpu.VMEM((1, flats), f32),
            pltpu.VMEM((owners * shards, 1, flats), f32),
            pltpu.VMEM((owners, COMPONENTS, rows), f32),
            pltpu.VMEM((rows, flats), bf16),
            pltpu.VMEM((flats, rows), bf16),
            pltpu.VMEM((tokens, depth), bf16),
            pltpu.VMEM((1, depth), f32),
            pltpu.VMEM((1, depth), f32),
            pltpu.VMEM((1, tokens), jnp.int32),
            pltpu.SMEM((owners,), jnp.int32),
            pltpu.SMEM((1,), jnp.int32),
            dma((6,)), dma((ring + 1,)),
            dma((owners,)), dma((chunks + 2,)),
            dma((shards - 1,)), dma((shards - 1,)),
            dma((1,)), dma((1,)), dma((1,)), dma((1,)), dma((1,)),
        ],
        compiler_params=pltpu.CompilerParams(
            collective_id=0, has_side_effects=True, vmem_limit_bytes=limit,
        ),
    )(
        far(hidden_rows[0]), far(norm_gain), far(norm_bias),
        far(target_ids.reshape(1, tokens)), far(ckpt_steps), components, far(unembed[0].T),
    )

    out, gram, target = pl.pallas_call(
        functools.partial(mix_kernel, across),
        grid=(STEPS,),
        in_specs=[vmem] * 4,
        out_specs=[pl.BlockSpec((out_rows, across), lambda j: (0, j)), vmem, vmem],
        out_shape=[
            jax.ShapeDtypeStruct((out_rows, width), bf16),
            jax.ShapeDtypeStruct((owners, owners), f32),
            jax.ShapeDtypeStruct((1, tokens), f32),
        ],
        compiler_params=pltpu.CompilerParams(
            dimension_semantics=("arbitrary",),
            vmem_limit_bytes=rows * across * STEPS * 2 + 12 * out_rows * across + (8 << 20),
        ),
    )(x, w2, gexp, target)
    return out.reshape(COMPONENTS, slab, width), gram, target


def solution(mesh):
    return jax.shard_map(
        functools.partial(per_device, mesh.shape["ckpt"], mesh.shape["vocab"]),
        mesh=mesh,
        in_specs=(
            P("ckpt", None, None),
            P("ckpt", None),
            P("ckpt", None),
            P("ckpt", None, "vocab"),
            P(),
            P(),
            P(),
        ),
        out_specs=(P(None, "ckpt", "vocab"), P(), P("ckpt", None)),
        check_vma=False,
    )
```

time: 55.8 us -> 53.2 us (0.953)
  Pallas kernels: 54.1 us -> 51.7 us
    pallas_call x2, Pallas kernels: 54.1 us -> 51.7 us  [the longest x1 49.2 us: per_device(): pl.pallas_call(functools.partial(gather_kernel, sizes), in_specs=[hbm] *...]
where the time goes in v1:
time: 53.2 us; the launch traced here: 53 us
  Pallas kernels  51.7 us (97%)
  between operations  1.29 us (2%)
    pallas_call x1, Pallas kernels, per_device(): pl.pallas_call(functools.partial(gather_kernel, sizes), in_specs=[hbm] *...  49.2 us
    pallas_call x1, Pallas kernels, per_device(): pl.pallas_call(functools.partial(mix_kernel, across), grid=(STEPS,), in_s...  2.56 us

profile of v1, /device:TPU:0, one launch (start us, length us, event | category | flops | bytes accessed | tf_op | source)
XLA Modules:
  0.0 53.0 jit_solution(11799237924215674280)
XLA Ops:
  1.3 49.2 %shard_map.94 = (bf16[128,12800]{1,0:T(8,128)(2,1)S(1)}, bf16[128,256]{1,0:T(8,128)(2,1)S(1)}, f32[8,128]{1,0:T(8,128)S(1)}, f32[1,128]{1,0:T(1,128)S(1)}) custom-call(bf16[128,768]{1,0:T(8,128)(2,1)} %bitcast.7, f32[1,768]{1,0:T(1,128)} %gain_hbm.1, f32[1,768]{1,0:T(1,128)} %bias_hbm.1, s32[1,128]{1,0:T(1,128)} %bitcast.8, s32[8]{0:T(128)} %steps_hbm.1, ...), custom_call_target="tpu_custom_call" | custom-call | tf_op jit(solution)/shard_map/pallas_call | solution.py:448
  50.5 2.6 %shard_map.95 = (bf16[128,12576]{1,0:T(8,128)(2,1)}, f32[8,8]{1,0:T(8,128)}, f32[1,128]{1,0:T(1,128)}) custom-call(bf16[128,12800]{1,0:T(8,128)(2,1)S(1)} %get-tuple-element.10.x_ref, bf16[128,256]{1,0:T(8,128)(2,1)S(1)} %get-tuple-element.11.w2_ref, f32[8,128]{1,0:T(8,128)S(1)} %get-tuple-element.12.gexp_ref, f32[1,128]{1,0:T(1,128)S(1)} %get-tuple-element.13.target_in), custom_call_target="tpu_custom_call" | custom-call | tf_op jit(solution)/shard_map/pallas_call | solution.py:496

commit v2 on v1

--- a/solution.py
+++ b/solution.py
@@ -14,7 +14,7 @@
 NT = (((1,), (1,)), ((), ()))
 RING = 4
 STEPS = 2
-HOLD = 4
+HOLD = 2
 
 
 def split_tiles(width):
@@ -50,12 +50,12 @@
 
 def gather_kernel(
     sizes,
-    hidden_hbm, gain_hbm, bias_hbm, ids_hbm, steps_hbm, comps_hbm, w_hbm,
+    hidden_hbm, gain_hbm, bias_hbm, ids_hbm, steps_hbm, comps_ref, w_hbm,
     xout_ref, w2_ref, gexp_ref, target_ref,
-    normed, wbuf, xsend, xrecv, off, ids, tops, sums, hits, stat, stats, dsend, drecv,
+    normed, wbuf, xsend, xrecv, off, ids, tops, sums, hits, stat, stats, dsend, drecv, dcol,
     gsend, grecv, basis, to_flat, from_flat,
-    hidden_ref, gain_ref, bias_ref, ids_ref, steps_ref, comps_ref, in_sem, wsem,
-    send_sem, recv_sem, ssend, srecv, dssem, drsem, gssem, grsem, out_sem,
+    hidden_ref, gain_ref, bias_ref, ids_ref, steps_ref, in_sem, wsem,
+    send_sem, recv_sem, ssend, srecv, dssem, drsem, gssem, grsem, out_sem, ready,
 ):
     owners, shards, tokens, width, tile, chunks = sizes
     slab = tokens // owners
@@ -91,19 +91,18 @@
     loads = []
     for i, (src, dst) in enumerate((
         (hidden_hbm, hidden_ref), (gain_hbm, gain_ref), (bias_hbm, bias_ref),
-        (ids_hbm, ids_ref), (steps_hbm, steps_ref), (comps_hbm, comps_ref),
+        (ids_hbm, ids_ref), (steps_hbm, steps_ref),
     )):
         loads.append(pltpu.make_async_copy(src, dst, in_sem.at[i]))
     for load in loads[:3]:
         load.start()
     fetch(0, 0, 0, cut).start()
     barrier = pltpu.get_barrier_semaphore()
-    for q in range(shards - 1, -1, -1):
-        for r in range(owners - 1, -1, -1):
-            if q or r:
-                pl.semaphore_signal(
-                    barrier, inc=1, device_id=(peer(r), side(q)), device_id_type=MESH
-                )
+    greeted = [(0, q) for q in range(1, shards)] + [(r, 0) for r in range(1, owners)]
+    for r, q in greeted:
+        pl.semaphore_signal(
+            barrier, inc=1, device_id=(peer(r), side(q)), device_id_type=MESH
+        )
     fetch(0, 0, cut, tile - cut, ring).start()
     for load in loads[3:]:
         load.start()
@@ -118,7 +117,7 @@
     centre = jnp.mean(floats, axis=1, keepdims=True)
     spread = jnp.mean((floats - centre) ** 2, axis=1, keepdims=True)
     normed[...] = (
-        (floats - centre) / jnp.sqrt(spread + 1e-05) * gain_ref[...] + bias_ref[...]
+        (floats - centre) * (1.0 / jnp.sqrt(spread + 1e-05)) * gain_ref[...] + bias_ref[...]
     ).astype(jnp.bfloat16)
     lane = iota((tokens, LANES), 1)
 
@@ -200,8 +199,10 @@
     )
     parts = split_parts(logits, 0, False)
     store(parts, 0)
-    pl.semaphore_wait(barrier, owners * shards - 1)
+    pl.semaphore_wait(barrier, owners + shards - 2)
     send(0, cut, 0)
+    for r in range(1, owners):
+        pl.semaphore_signal(ready, inc=1, device_id=(peer(r), mine), device_id_type=MESH)
     for load in loads[3:]:
         load.wait()
     wide = jnp.broadcast_to(ids_ref[...].astype(jnp.float32), (LANES, tokens))
@@ -257,7 +258,12 @@
     top = jnp.max(tops[...], axis=1, keepdims=True)
     total = jnp.sum(sums[...] * jnp.exp(tops[...] - top), axis=1, keepdims=True)
     picked = jnp.sum(hits[...], axis=1, keepdims=True)
-    stat[...] = jnp.where(lane == 0, top, jnp.where(lane == 1, total, picked))
+    stat[...] = jnp.transpose(
+        jnp.where(
+            lane == 0, top,
+            jnp.where(lane == 1, total, jnp.where(lane == 2, picked, off[...])),
+        )
+    )[0:8, :]
     sent = []
     for r in range(1, shards):
         copy = pltpu.make_async_remote_copy(
@@ -289,26 +295,26 @@
 
     for copy in sent:
         copy.wait()
-    best = top
+    best = stat[0:1, :]
     for r in range(shards - 1):
-        best = jnp.maximum(best, stats[r][:, 0:1])
-    total = total * jnp.exp(top - best)
+        best = jnp.maximum(best, stats[r][0:1, :])
+    total = stat[1:2, :] * jnp.exp(stat[0:1, :] - best)
+    picked = stat[2:3, :]
     for r in range(shards - 1):
-        total = total + stats[r][:, 1:2] * jnp.exp(stats[r][:, 0:1] - best)
-        picked = picked + stats[r][:, 2:3]
+        total = total + stats[r][1:2, :] * jnp.exp(stats[r][0:1, :] - best)
+        picked = picked + stats[r][2:3, :]
     lse = best + jnp.log(total)
-    dsend[...] = jnp.broadcast_to(off[:, 0:1] - lse, dsend.shape)
+    dsend[...] = stat[3:4, :] - lse
     for r in range(1, owners):
-        to = peer(r)
         pltpu.make_async_remote_copy(
-            src_ref=dsend.at[pl.ds(pl.multiple_of(to * slab, slab), slab), :],
-            dst_ref=drecv.at[my_rows, :],
+            src_ref=dsend,
+            dst_ref=drecv.at[me],
             send_sem=dssem.at[0],
             recv_sem=drsem.at[0],
-            device_id=(to, mine),
+            device_id=(peer(r), mine),
             device_id_type=MESH,
         ).start()
-    pltpu.make_async_copy(dsend.at[my_rows, :], drecv.at[my_rows, :], drsem.at[0]).start()
+    pltpu.make_async_copy(dsend, drecv.at[me], drsem.at[0]).start()
 
     def late(j, carry):
         send(j * tile, tile, j + 1)
@@ -317,19 +323,19 @@
     lax.fori_loop(held, last, late, 0)
     send(tail_at, tile - cut, chunks)
     send(tail_at + tile - cut, cut, chunks + 1)
-    target_ref[...] = jnp.transpose(
-        jnp.broadcast_to(picked - lse, (tokens, LANES))
-    )[0:1, :]
+    target_ref[...] = picked - lse
 
     pltpu.make_async_copy(drecv, drecv, drsem.at[0]).wait()
-    d = drecv[...].reshape(owners, slab, LANES)
-    d = d - jnp.mean(d, axis=0, keepdims=True)
-    drecv[...] = d.reshape(rows, LANES)
+    d = drecv[...]
+    d = jnp.broadcast_to(d - jnp.mean(d, axis=0, keepdims=True), (owners, slab, tokens))
+    here = iota(d.shape, 2) == me * slab + iota(d.shape, 1)
+    d = jnp.sum(jnp.where(here, d, 0.0), axis=2, keepdims=True)
+    dcol[...] = jnp.broadcast_to(d, (owners, slab, LANES)).reshape(rows, LANES)
 
     def absorb(start, count, piece, products, edge=False):
         block = xrecv.at[:, columns(start, count)]
         pltpu.make_async_copy(block, block, recv_sem.at[piece]).wait()
-        level = drecv[...].reshape(owners, slab, LANES)
+        level = dcol[...].reshape(owners, slab, LANES)
         for g in range(count // LANES):
             at = columns(start + g * LANES, LANES)
             x = xrecv[:, at].astype(jnp.float32).reshape(owners, slab, LANES)
@@ -358,23 +364,26 @@
         jnp.where(flat_own, select_sum(partial, to_flat[...]), 0.0), axis=0, keepdims=True
     )
     slot = mine * owners + me
-    for q in range(shards - 1, -1, -1):
-        for r in range(owners - 1, -1, -1):
-            if q or r:
+    pl.semaphore_wait(ready, owners - 1)
+    for q in range(shards):
+        for r in range(owners):
+            @pl.when(slot != q * owners + r)
+            def _(q=q, r=r):
                 pltpu.make_async_remote_copy(
                     src_ref=gsend,
                     dst_ref=grecv.at[slot],
                     send_sem=gssem.at[0],
                     recv_sem=grsem.at[0],
-                    device_id=(peer(r), side(q)),
+                    device_id=(jnp.int32(r), jnp.int32(q)),
                     device_id_type=MESH,
                 ).start()
+
     pltpu.make_async_copy(gsend, grecv.at[slot], grsem.at[0]).start()
     for r in range(1, owners):
         strip = xsend.at[my_rows, :]
         pltpu.make_async_copy(strip, strip, send_sem.at[r]).wait()
-    others = pl.ds(0, rows - slab)
-    pltpu.make_async_copy(dsend.at[others, :], dsend.at[others, :], dssem.at[0]).wait()
+    others = pl.ds(0, owners - 1)
+    pltpu.make_async_copy(drecv.at[others], drecv.at[others], dssem.at[0]).wait()
     row_k = iota((kinds, slab, rows), 0)
     keep = (iota((kinds, slab, rows), 2) % slab == iota((kinds, slab, rows), 1)) & (
         row_k < comps_ref[0]
@@ -447,7 +456,7 @@
 
     x, w2, gexp, target = pl.pallas_call(
         functools.partial(gather_kernel, sizes),
-        in_specs=[hbm] * 7,
+        in_specs=[hbm] * 5 + [pl.BlockSpec(memory_space=pltpu.SMEM), hbm],
         out_specs=[pl.BlockSpec(memory_space=pl.ANY), vmem, vmem, vmem],
         out_shape=[
             jax.ShapeDtypeStruct((rows, across * STEPS), bf16),
@@ -465,9 +474,10 @@
             pltpu.VMEM((tokens, LANES), f32),
             pltpu.VMEM((tokens, LANES), f32),
             pltpu.VMEM((tokens, LANES), f32),
-            pltpu.VMEM((tokens, LANES), f32),
-            pltpu.VMEM((shards - 1, tokens, LANES), f32),
-            pltpu.VMEM((tokens, LANES), f32),
+            pltpu.VMEM((8, tokens), f32),
+            pltpu.VMEM((shards - 1, 8, tokens), f32),
+            pltpu.VMEM((1, tokens), f32),
+            pltpu.VMEM((owners, 1, tokens), f32),
             pltpu.VMEM((rows, LANES), f32),
             pltpu.VMEM((1, flats), f32),
             pltpu.VMEM((owners * shards, 1, flats), f32),
@@ -479,11 +489,11 @@
             pltpu.VMEM((1, depth), f32),
             pltpu.VMEM((1, tokens), jnp.int32),
             pltpu.SMEM((owners,), jnp.int32),
-            pltpu.SMEM((1,), jnp.int32),
-            dma((6,)), dma((ring + 1,)),
+            dma((5,)), dma((ring + 1,)),
             dma((owners,)), dma((chunks + 2,)),
             dma((shards - 1,)), dma((shards - 1,)),
             dma((1,)), dma((1,)), dma((1,)), dma((1,)), dma((1,)),
+            pltpu.SemaphoreType.REGULAR,
         ],
         compiler_params=pltpu.CompilerParams(
             collective_id=0, has_side_effects=True, vmem_limit_bytes=limit,

time: 53.2 us -> 52.2 us (0.981)
  Pallas kernels: 51.7 us -> 50.7 us
    pallas_call x1, Pallas kernels: 49.2 us -> 48.2 us  [per_device(): pl.pallas_call(functools.partial(gather_kernel, sizes), in_specs=[hbm] *...]
where the time goes in v2:
time: 52.2 us; the launch traced here: 52 us
  Pallas kernels  50.7 us (97%)
  between operations  1.29 us (2%)
    pallas_call x1, Pallas kernels, per_device(): pl.pallas_call(functools.partial(gather_kernel, sizes), in_specs=[hbm] *...  48.2 us
    pallas_call x1, Pallas kernels, per_device(): pl.pallas_call(functools.partial(mix_kernel, across), grid=(STEPS,), in_s...  2.55 us

profile of v2, /device:TPU:0, one launch (start us, length us, event | category | flops | bytes accessed | tf_op | source)
XLA Modules:
  0.0 52.0 jit_solution(15514329686825361339)
XLA Ops:
  1.3 48.2 %shard_map.94 = (bf16[128,12800]{1,0:T(8,128)(2,1)S(1)}, bf16[128,256]{1,0:T(8,128)(2,1)S(1)}, f32[8,128]{1,0:T(8,128)S(1)}, f32[1,128]{1,0:T(1,128)S(1)}) custom-call(bf16[128,768]{1,0:T(8,128)(2,1)} %bitcast.7, f32[1,768]{1,0:T(1,128)} %gain_hbm.1, f32[1,768]{1,0:T(1,128)} %bias_hbm.1, s32[1,128]{1,0:T(1,128)} %bitcast.8, s32[8]{0:T(128)} %steps_hbm.1, ...), custom_call_target="tpu_custom_call" | custom-call | tf_op jit(solution)/shard_map/pallas_call | solution.py:457
  49.5 2.5 %shard_map.95 = (bf16[128,12576]{1,0:T(8,128)(2,1)}, f32[8,8]{1,0:T(8,128)}, f32[1,128]{1,0:T(1,128)}) custom-call(bf16[128,12800]{1,0:T(8,128)(2,1)S(1)} %get-tuple-element.10.x_ref, bf16[128,256]{1,0:T(8,128)(2,1)S(1)} %get-tuple-element.11.w2_ref, f32[8,128]{1,0:T(8,128)S(1)} %get-tuple-element.12.gexp_ref, f32[1,128]{1,0:T(1,128)S(1)} %get-tuple-element.13.target_in), custom_call_target="tpu_custom_call" | custom-call | tf_op jit(solution)/shard_map/pallas_call | solution.py:506

commit v3 on v2

--- a/solution.py
+++ b/solution.py
@@ -13,7 +13,6 @@
 LOW = -1e30
 NT = (((1,), (1,)), ((), ()))
 RING = 4
-STEPS = 2
 HOLD = 2
 
 
@@ -407,30 +406,59 @@
     w2_ref[:, 0:rows] = high
     w2_ref[:, rows:] = low
     gexp_ref[...] = gexp
-    pltpu.make_async_copy(xrecv, xout_ref.at[:, columns(0, tile * chunks)], out_sem.at[0]).wait()
+    pltpu.make_async_copy(xrecv, xout_ref, out_sem.at[0]).wait()
     less = pl.ds(0, owners * shards - 1)
     pltpu.make_async_copy(grecv.at[less], grecv.at[less], gssem.at[0]).wait()
 
 
-def mix_kernel(across, x_ref, w2_ref, gexp_ref, target_in, out_ref, gram_ref, target_ref):
-    start = pl.multiple_of(pl.program_id(0) * across, LANES)
-    x = x_ref[:, pl.ds(start, across)]
-    out_ref[...] = jnp.dot(
-        w2_ref[...], jnp.concatenate([x, x], axis=0), preferred_element_type=jnp.float32
-    ).astype(jnp.bfloat16)
-
-    @pl.when(pl.program_id(0) == pl.num_programs(0) - 1)
-    def _():
+def mix_pieces(tiles):
+    pieces = []
+    for most in [6, 12] + [18] * tiles:
+        if tiles:
+            pieces.append(min(most, tiles))
+            tiles -= pieces[-1]
+    return pieces
+
+
+def mix_kernel(
+    width, x_ref, w2_ref, gexp_ref, target_in, out_ref, gram_ref, target_ref,
+    held, gram, sem, small_sem,
+):
+    at = 0
+    copies = [pltpu.make_async_copy(target_in, target_ref, small_sem.at[0])]
+    copies[0].start()
+
+    def send_gram():
         owners, rows = gexp_ref.shape
         pick = (
             lax.broadcasted_iota(jnp.int32, (rows, LANES), 0)
             == lax.broadcasted_iota(jnp.int32, (rows, LANES), 1) * (rows // owners)
         ).astype(jnp.float32)
-        gram_ref[...] = jnp.dot(
+        gram[...] = jnp.dot(
             gexp_ref[...], pick, precision=lax.Precision.HIGHEST,
             preferred_element_type=jnp.float32,
         )[:, :owners]
-        target_ref[...] = target_in[...]
+        copies.append(pltpu.make_async_copy(gram, gram_ref, small_sem.at[1]))
+        copies[-1].start()
+
+    pieces = mix_pieces(held.shape[1] // LANES)
+    for i, tiles in enumerate(pieces):
+        if i == min(3, len(pieces) - 1):
+            send_gram()
+        count = tiles * LANES
+        x = x_ref[:, at:at + count]
+        held[:, at:at + count] = jnp.dot(
+            w2_ref[...], jnp.concatenate([x, x], axis=0), preferred_element_type=jnp.float32
+        ).astype(jnp.bfloat16)
+        span = pl.ds(at, count)
+        if at + count > width:
+            span = pl.ds(at, pl.multiple_of(count + pl.program_id(0) * LANES, LANES))
+        copy = pltpu.make_async_copy(held.at[:, span], out_ref.at[:, span], sem.at[i])
+        copy.start()
+        copies.append(copy)
+        at += count
+    for copy in copies:
+        copy.wait()
 
 
 def per_device(owners, shards, hidden_rows, norm_gain, norm_bias, unembed, target_ids, ckpt_steps, components):
@@ -441,7 +469,6 @@
     out_rows = COMPONENTS * slab
     tile, chunks = split_tiles(width)
     padded = tile * chunks
-    across = -(-(padded // LANES) // STEPS) * LANES
     flats = max(owners * owners, LANES)
     ring = min(RING, chunks)
     sizes = (owners, shards, tokens, width, tile, chunks)
@@ -459,7 +486,7 @@
         in_specs=[hbm] * 5 + [pl.BlockSpec(memory_space=pltpu.SMEM), hbm],
         out_specs=[pl.BlockSpec(memory_space=pl.ANY), vmem, vmem, vmem],
         out_shape=[
-            jax.ShapeDtypeStruct((rows, across * STEPS), bf16),
+            jax.ShapeDtypeStruct((rows, padded), bf16),
             jax.ShapeDtypeStruct((out_rows, 2 * rows), bf16),
             jax.ShapeDtypeStruct((owners, rows), f32),
             jax.ShapeDtypeStruct((1, tokens), f32),
@@ -504,18 +531,23 @@
     )
 
     out, gram, target = pl.pallas_call(
-        functools.partial(mix_kernel, across),
-        grid=(STEPS,),
+        functools.partial(mix_kernel, width),
+        grid=(1,),
         in_specs=[vmem] * 4,
-        out_specs=[pl.BlockSpec((out_rows, across), lambda j: (0, j)), vmem, vmem],
+        out_specs=[hbm, hbm, hbm],
         out_shape=[
             jax.ShapeDtypeStruct((out_rows, width), bf16),
             jax.ShapeDtypeStruct((owners, owners), f32),
             jax.ShapeDtypeStruct((1, tokens), f32),
         ],
+        scratch_shapes=[
+            pltpu.VMEM((out_rows, padded), bf16),
+            pltpu.VMEM((owners, owners), f32),
+            dma((len(mix_pieces(padded // LANES)),)), dma((2,)),
+        ],
         compiler_params=pltpu.CompilerParams(
             dimension_semantics=("arbitrary",),
-            vmem_limit_bytes=rows * across * STEPS * 2 + 12 * out_rows * across + (8 << 20),
+            vmem_limit_bytes=2 * (rows + out_rows) * padded + (16 << 20),
         ),
     )(x, w2, gexp, target)
     return out.reshape(COMPONENTS, slab, width), gram, target

time: 52.2 us -> 51.7 us (level)
  no operation moved by 1% of the time
where the time goes in v3:
time: 51.7 us; the launch traced here: 51.5 us
  Pallas kernels  50.3 us (97%)
  between operations  1.29 us (2%)
    pallas_call x1, Pallas kernels, per_device(): pl.pallas_call(functools.partial(gather_kernel, sizes), in_specs=[hbm] *...  48.2 us
    pallas_call x1, Pallas kernels, per_device(): pl.pallas_call(functools.partial(mix_kernel, width), grid=(1,), in_specs=...  2.09 us

profile of v3, /device:TPU:0, one launch (start us, length us, event | category | flops | bytes accessed | tf_op | source)
XLA Modules:
  0.0 51.5 jit_solution(9141838886228829188)
XLA Ops:
  1.3 48.2 %shard_map.94 = (bf16[128,12672]{1,0:T(8,128)(2,1)S(1)}, bf16[128,256]{1,0:T(8,128)(2,1)S(1)}, f32[8,128]{1,0:T(8,128)S(1)}, f32[1,128]{1,0:T(1,128)S(1)}) custom-call(bf16[128,768]{1,0:T(8,128)(2,1)} %bitcast.7, f32[1,768]{1,0:T(1,128)} %gain_hbm.1, f32[1,768]{1,0:T(1,128)} %bias_hbm.1, s32[1,128]{1,0:T(1,128)} %bitcast.8, s32[8]{0:T(128)} %steps_hbm.1, ...), custom_call_target="tpu_custom_call" | custom-call | tf_op jit(solution)/shard_map/pallas_call | solution.py:484
  49.5 2.1 %shard_map.95 = (bf16[128,12576]{1,0:T(8,128)(2,1)}, f32[8,8]{1,0:T(8,128)}, f32[1,128]{1,0:T(1,128)}) custom-call(bf16[128,12672]{1,0:T(8,128)(2,1)S(1)} %get-tuple-element.10.x_ref, bf16[128,256]{1,0:T(8,128)(2,1)S(1)} %get-tuple-element.11.w2_ref, f32[8,128]{1,0:T(8,128)S(1)} %get-tuple-element.12.gexp_ref, f32[1,128]{1,0:T(1,128)S(1)} %get-tuple-element.13.target_in), custom_call_target="tpu_custom_call" | custom-call | tf_op jit(solution)/shard_map/pallas_call | solution.py:533

commit v4 on v3

--- a/solution.py
+++ b/solution.py
@@ -14,6 +14,8 @@
 NT = (((1,), (1,)), ((), ()))
 RING = 4
 HOLD = 2
+DETOUR = 2
+DETOUR_TILES = 3
 
 
 def split_tiles(width):
@@ -51,10 +53,10 @@
     sizes,
     hidden_hbm, gain_hbm, bias_hbm, ids_hbm, steps_hbm, comps_ref, w_hbm,
     xout_ref, w2_ref, gexp_ref, target_ref,
-    normed, wbuf, xsend, xrecv, off, ids, tops, sums, hits, stat, stats, dsend, drecv, dcol,
+    normed, wbuf, xsend, xrecv, off, ids, tops, sums, hits, stat, stats, dsend, drecv, dcol, relay,
     gsend, grecv, basis, to_flat, from_flat,
     hidden_ref, gain_ref, bias_ref, ids_ref, steps_ref, in_sem, wsem,
-    send_sem, recv_sem, ssend, srecv, dssem, drsem, gssem, grsem, out_sem, ready,
+    send_sem, recv_sem, ssend, srecv, dssem, drsem, gssem, grsem, out_sem, ready, rssem, rrsem, fsem,
 ):
     owners, shards, tokens, width, tile, chunks = sizes
     slab = tokens // owners
@@ -74,6 +76,12 @@
 
     def side(r):
         return lax.rem(mine + r, shards)
+
+    detour = relay.shape[1]
+    held = max(1, last - HOLD)
+    detouring = shards > 1 and held > DETOUR
+    first_shard = (mine == 0) & detouring
+    last_shard = (mine == shards - 1) & detouring
 
     def iota(shape, axis):
         return lax.broadcasted_iota(jnp.int32, shape, axis)
@@ -147,6 +155,13 @@
                 value = jnp.where(inside, value, 0.0)
             xsend[:, columns(start + g * LANES, LANES)] = value.astype(jnp.bfloat16)
 
+    def keep_own(start, count, piece):
+        pltpu.make_async_copy(
+            xsend.at[my_rows, columns(start, count)],
+            xrecv.at[my_rows, columns(start, count)],
+            recv_sem.at[piece],
+        ).start()
+
     def send(start, count, piece):
         for r in range(1, owners):
             to = peer(r)
@@ -160,11 +175,22 @@
                 device_id=(to, mine),
                 device_id_type=MESH,
             ).start()
-        pltpu.make_async_copy(
-            xsend.at[my_rows, columns(start, count)],
-            xrecv.at[my_rows, columns(start, count)],
-            recv_sem.at[piece],
-        ).start()
+        keep_own(start, count, piece)
+
+    def forward():
+        start = DETOUR * tile
+        several = relay.at[pl.ds(0, rows - slab), :]
+        pltpu.make_async_copy(several, several, rrsem.at[0]).wait()
+        for r in range(1, owners):
+            strip = pl.ds(pl.multiple_of(peer(r) * slab, slab), slab)
+            pltpu.make_async_remote_copy(
+                src_ref=relay.at[strip, :],
+                dst_ref=xrecv.at[strip, columns(start, detour)],
+                send_sem=fsem.at[0],
+                recv_sem=recv_sem.at[DETOUR + 1],
+                device_id=(me, jnp.int32(shards - 1)),
+                device_id_type=MESH,
+            ).start()
 
     def gather_stats(parts, start):
         old_top = tops[...]
@@ -202,6 +228,11 @@
     send(0, cut, 0)
     for r in range(1, owners):
         pl.semaphore_signal(ready, inc=1, device_id=(peer(r), mine), device_id_type=MESH)
+    fetch(0, 0, cut, tile - cut, ring).wait()
+    more = logits_of(0, cut, tile - cut)
+    more_parts = split_parts(more, cut, False)
+    store(more_parts, cut)
+    send(cut, tile - cut, 1)
     for load in loads[3:]:
         load.wait()
     wide = jnp.broadcast_to(ids_ref[...].astype(jnp.float32), (LANES, tokens))
@@ -209,12 +240,6 @@
     tops[...] = jnp.full_like(tops, LOW)
     sums[...] = jnp.zeros_like(sums)
     hits[...] = jnp.zeros_like(hits)
-
-    fetch(0, 0, cut, tile - cut, ring).wait()
-    more = logits_of(0, cut, tile - cut)
-    more_parts = split_parts(more, cut, False)
-    store(more_parts, cut)
-    send(cut, tile - cut, 1)
     gather_stats(parts, 0)
     gather_stats(more_parts, cut)
     if ring == last:
@@ -222,7 +247,7 @@
     elif ring < last:
         fetch(ring, 0).start()
 
-    held = max(1, last - HOLD)
+    pl.semaphore_wait(ready, owners - 1)
 
     def middle(j, carry):
         slot = lax.rem(j, ring)
@@ -231,9 +256,26 @@
         chunk_parts = split_parts(logits_of(slot, 0, tile), start, False)
         store(chunk_parts, start)
 
-        @pl.when(j < held)
+        @pl.when((j < held) & jnp.logical_not(last_shard & (j == DETOUR)))
         def _():
             send(start, tile, j + 1)
+
+        @pl.when(last_shard & (j == DETOUR))
+        def _():
+            keep_own(start, detour, j + 1)
+            for r in range(1, owners):
+                to = peer(r)
+                pltpu.make_async_remote_copy(
+                    src_ref=xsend.at[
+                        pl.ds(pl.multiple_of(to * slab, slab), slab), columns(start, detour)
+                    ],
+                    dst_ref=relay.at[my_rows, :],
+                    send_sem=rssem.at[0],
+                    recv_sem=rrsem.at[0],
+                    device_id=(to, jnp.int32(0)),
+                    device_id_type=MESH,
+                ).start()
+            send(start + detour, tile - detour, j + 1)
 
         gather_stats(chunk_parts, start)
 
@@ -322,6 +364,7 @@
     lax.fori_loop(held, last, late, 0)
     send(tail_at, tile - cut, chunks)
     send(tail_at + tile - cut, cut, chunks + 1)
+    pl.when(first_shard)(forward)
     target_ref[...] = picked - lse
 
     pltpu.make_async_copy(drecv, drecv, drsem.at[0]).wait()
@@ -363,7 +406,6 @@
         jnp.where(flat_own, select_sum(partial, to_flat[...]), 0.0), axis=0, keepdims=True
     )
     slot = mine * owners + me
-    pl.semaphore_wait(ready, owners - 1)
     for q in range(shards):
         for r in range(owners):
             @pl.when(slot != q * owners + r)
@@ -378,9 +420,25 @@
                 ).start()
 
     pltpu.make_async_copy(gsend, grecv.at[slot], grsem.at[0]).start()
-    for r in range(1, owners):
-        strip = xsend.at[my_rows, :]
-        pltpu.make_async_copy(strip, strip, send_sem.at[r]).wait()
+    @pl.when(last_shard)
+    def _():
+        several = relay.at[pl.ds(0, rows - slab), :]
+        pltpu.make_async_copy(several, several, rssem.at[0]).wait()
+        for r in range(1, owners):
+            strip = xsend.at[my_rows, columns(0, tile * chunks - detour)]
+            pltpu.make_async_copy(strip, strip, send_sem.at[r]).wait()
+
+    @pl.when(jnp.logical_not(last_shard))
+    def _():
+        for r in range(1, owners):
+            strip = xsend.at[my_rows, :]
+            pltpu.make_async_copy(strip, strip, send_sem.at[r]).wait()
+
+    @pl.when(first_shard)
+    def _():
+        sent_on = relay.at[pl.ds(0, rows - slab), :]
+        pltpu.make_async_copy(sent_on, sent_on, fsem.at[0]).wait()
+
     others = pl.ds(0, owners - 1)
     pltpu.make_async_copy(drecv.at[others], drecv.at[others], dssem.at[0]).wait()
     row_k = iota((kinds, slab, rows), 0)
@@ -506,6 +564,7 @@
             pltpu.VMEM((1, tokens), f32),
             pltpu.VMEM((owners, 1, tokens), f32),
             pltpu.VMEM((rows, LANES), f32),
+            pltpu.VMEM((tokens, DETOUR_TILES * LANES), bf16),
             pltpu.VMEM((1, flats), f32),
             pltpu.VMEM((owners * shards, 1, flats), f32),
             pltpu.VMEM((owners, COMPONENTS, rows), f32),
@@ -520,7 +579,7 @@
             dma((owners,)), dma((chunks + 2,)),
             dma((shards - 1,)), dma((shards - 1,)),
             dma((1,)), dma((1,)), dma((1,)), dma((1,)), dma((1,)),
-            pltpu.SemaphoreType.REGULAR,
+            pltpu.SemaphoreType.REGULAR, dma((1,)), dma((1,)), dma((1,)),
         ],
         compiler_params=pltpu.CompilerParams(
             collective_id=0, has_side_effects=True, vmem_limit_bytes=limit,

time: 51.7 us -> 50.8 us (0.983)
  Pallas kernels: 50.3 us -> 49.4 us
    pallas_call x1, Pallas kernels: 48.2 us -> 47.3 us  [per_device(): pl.pallas_call(functools.partial(gather_kernel, sizes), in_specs=[hbm] *...]
where the time goes in v4:
time: 50.8 us; the launch traced here: 50.6 us
  Pallas kernels  49.4 us (97%)
  between operations  1.29 us (3%)
    pallas_call x1, Pallas kernels, per_device(): pl.pallas_call(functools.partial(gather_kernel, sizes), in_specs=[hbm] *...  47.3 us
    pallas_call x1, Pallas kernels, per_device(): pl.pallas_call(functools.partial(mix_kernel, width), grid=(1,), in_specs=...  2.08 us

profile of v4, /device:TPU:0, one launch (start us, length us, event | category | flops | bytes accessed | tf_op | source)
XLA Modules:
  0.0 50.6 jit_solution(9999717465411075836)
XLA Ops:
  1.3 47.3 %shard_map.94 = (bf16[128,12672]{1,0:T(8,128)(2,1)S(1)}, bf16[128,256]{1,0:T(8,128)(2,1)S(1)}, f32[8,128]{1,0:T(8,128)S(1)}, f32[1,128]{1,0:T(1,128)S(1)}) custom-call(bf16[128,768]{1,0:T(8,128)(2,1)} %bitcast.7, f32[1,768]{1,0:T(1,128)} %gain_hbm.1, f32[1,768]{1,0:T(1,128)} %bias_hbm.1, s32[1,128]{1,0:T(1,128)} %bitcast.8, s32[8]{0:T(128)} %steps_hbm.1, ...), custom_call_target="tpu_custom_call" | custom-call | tf_op jit(solution)/shard_map/pallas_call | solution.py:542
  48.6 2.1 %shard_map.95 = (bf16[128,12576]{1,0:T(8,128)(2,1)}, f32[8,8]{1,0:T(8,128)}, f32[1,128]{1,0:T(1,128)}) custom-call(bf16[128,12672]{1,0:T(8,128)(2,1)S(1)} %get-tuple-element.10.x_ref, bf16[128,256]{1,0:T(8,128)(2,1)S(1)} %get-tuple-element.11.w2_ref, f32[8,128]{1,0:T(8,128)S(1)} %get-tuple-element.12.gexp_ref, f32[1,128]{1,0:T(1,128)S(1)} %get-tuple-element.13.target_in), custom_call_target="tpu_custom_call" | custom-call | tf_op jit(solution)/shard_map/pallas_call | solution.py:592

commit v5 on v4

--- a/solution.py
+++ b/solution.py
@@ -63,7 +63,7 @@
     rows = owners * slab
     kinds = COMPONENTS
     ring = wbuf.shape[0]
-    cut = (tile // LANES // 3) * LANES
+    cut = (tile // LANES // 2) * LANES
     flats = gsend.shape[1]
     me = lax.axis_index("ckpt")
     mine = lax.axis_index("vocab")

time: 50.8 us -> 50.8 us (level)
  no operation moved by 1% of the time
where the time goes in v5:
time: 50.8 us; the launch traced here: 50.7 us
  Pallas kernels  49.4 us (97%)
  between operations  1.29 us (3%)
    pallas_call x1, Pallas kernels, per_device(): pl.pallas_call(functools.partial(gather_kernel, sizes), in_specs=[hbm] *...  47.3 us
    pallas_call x1, Pallas kernels, per_device(): pl.pallas_call(functools.partial(mix_kernel, width), grid=(1,), in_specs=...  2.09 us

profile of v5, /device:TPU:0, one launch (start us, length us, event | category | flops | bytes accessed | tf_op | source)
XLA Modules:
  0.0 50.7 jit_solution(4737056857207623260)
XLA Ops:
  1.3 47.3 %shard_map.94 = (bf16[128,12672]{1,0:T(8,128)(2,1)S(1)}, bf16[128,256]{1,0:T(8,128)(2,1)S(1)}, f32[8,128]{1,0:T(8,128)S(1)}, f32[1,128]{1,0:T(1,128)S(1)}) custom-call(bf16[128,768]{1,0:T(8,128)(2,1)} %bitcast.7, f32[1,768]{1,0:T(1,128)} %gain_hbm.1, f32[1,768]{1,0:T(1,128)} %bias_hbm.1, s32[1,128]{1,0:T(1,128)} %bitcast.8, s32[8]{0:T(128)} %steps_hbm.1, ...), custom_call_target="tpu_custom_call" | custom-call | tf_op jit(solution)/shard_map/pallas_call | solution.py:542
  48.6 2.1 %shard_map.95 = (bf16[128,12576]{1,0:T(8,128)(2,1)}, f32[8,8]{1,0:T(8,128)}, f32[1,128]{1,0:T(1,128)}) custom-call(bf16[128,12672]{1,0:T(8,128)(2,1)S(1)} %get-tuple-element.10.x_ref, bf16[128,256]{1,0:T(8,128)(2,1)S(1)} %get-tuple-element.11.w2_ref, f32[8,128]{1,0:T(8,128)S(1)} %get-tuple-element.12.gexp_ref, f32[1,128]{1,0:T(1,128)S(1)} %get-tuple-element.13.target_in), custom_call_target="tpu_custom_call" | custom-call | tf_op jit(solution)/shard_map/pallas_call | solution.py:592
